TPU v7x, 32 devices: a whole 2x2x4 slice. The times are simulated.
32 devices in a mesh: dp: 8 (over y, x, core), mp: 4 (over z).
Axes of the slice: x: 2, y: 2, z: 4, core: 2. Of those that a mesh axis runs over, the one named last changes fastest.
Arguments:
- tokens: bfloat16 [8, 2048, 512], P('dp', 'mp'), may hold values from -6 to 6
- cotangent: bfloat16 [8, 2048, 512], P('dp', 'mp'), may hold values from -6 to 6
- lengths: int32 [8], P('dp'), may hold values from 512 to 2048, as said below
- owners: int32 [96], replicated, may hold values from 0 to 7, as said below
- w_qkv: bfloat16 [512, 1536], P(None, 'mp'), may hold values from -0.25 to 0.25
- w_out: bfloat16 [512, 512], P('mp'), may hold values from -0.75 to 0.75
- w_in: bfloat16 [512, 2048], P(None, 'mp'), may hold values from -0.25 to 0.25
- w_down: bfloat16 [2048, 512], P('mp'), may hold values from -0.125 to 0.125
- master: float32 [192, 256, 128], P('dp', 'mp'), may hold values from -0.75 to 0.75
- first_moment: float32 [192, 256, 128], P('dp', 'mp'), may hold values from -28 to 28
- second_moment: float32 [192, 256, 128], P('dp', 'mp'), may hold values from 49.152 to 409.6
- norm_gains: float32 [2, 512], replicated, may hold values from 0.25 to 1.75
- norm_biases: float32 [2, 512], replicated, may hold values from -1.5 to 1.5
- norm_first: float32 [4, 512], replicated, may hold values from -64 to 64
- norm_second: float32 [4, 512], replicated, may hold values from 262.144 to 2064.384
Outputs:
- outputs: bfloat16 [8, 2048, 512], P('dp', 'mp')
- tokens_grad: float32 [8, 2048, 512], P('dp', 'mp')
- first_new: float32 [192, 256, 128], P('dp', 'mp')
- second_new: float32 [192, 256, 128], P('dp', 'mp')
- master_new: float32 [192, 256, 128], P('dp', 'mp')
- new_qkv: bfloat16 [512, 1536], P(None, 'mp')
- new_out: bfloat16 [512, 512], P('mp')
- new_in: bfloat16 [512, 2048], P(None, 'mp')
- new_down: bfloat16 [2048, 512], P('mp')
- norm_first_new: float32 [4, 512], replicated
- norm_second_new: float32 [4, 512], replicated
- norm_new: float32 [4, 512], replicated
Inputs may be any that keep to these rules, and one draw needn't show every extreme that they name: `lengths`: one sequence in every draw has all 2048 positions valid. `owners`: no owner holds more than 24 blocks and one owner holds exactly 24.
All inputs are finite; a program needn't handle non-finite values.
Results may differ from a plain program's by a relative error of at most 0.0097.
Values may be sent and summed in bfloat16 or wider, within the bound.
No kernel may reach another device: no remote copies, remote signals or barrier semaphores. Data moves between devices by JAX's collectives and lax.ppermute only.
A program may use at most 128 MiB of HBM per device.

v0:
```python
import jax
import jax.numpy as jnp
from jax import lax
from jax.sharding import PartitionSpec as P

HEAD = 64
BAND = 30
MARGIN = 32
QBLOCK = 512
STEP = 10
highest = lax.Precision.HIGHEST
learn_rate = 0.1
norm_rate = 0.3
decay_rate = 0.1
beta_one = 0.9
beta_two = 0.95
adam_epsilon = 1e-08
norm_epsilon = 1e-05


def layer_norm(values, scale_gain, shift_bias):
    row_mean = jnp.mean(values, axis=-1, keepdims=True)
    centered = values - row_mean
    variance = jnp.mean(centered * centered, axis=-1, keepdims=True)
    return centered * lax.rsqrt(variance + norm_epsilon) * scale_gain + shift_bias


def far_field(query, keys, values, key_mask, valid_count):
    masked = key_mask[:, None, None]
    feat_keys = (jax.nn.elu(keys) + 1.0) * masked
    tanh_keys = jnp.tanh(keys) * masked
    feat_query = jax.nn.elu(query) + 1.0
    tanh_query = jnp.tanh(query)
    state_one = jnp.einsum("lhe,lhf->hef", feat_keys, values, precision=highest)
    normaliser = jnp.sum(feat_keys, axis=0)
    denominator = jnp.einsum("lhe,he->lh", feat_query, normaliser, precision=highest)
    first_part = (
        jnp.einsum("lhe,hef->lhf", feat_query, state_one, precision=highest)
        / denominator[:, :, None]
    )
    state_two = jnp.einsum("lhe,lhf->hef", tanh_keys, values, precision=highest) / valid_count
    return first_part + jnp.einsum("lhe,hef->lhf", tanh_query, state_two, precision=highest)


def band_mask(anchor, length, seq_len, block):
    query_pos = anchor + jnp.arange(block, dtype=jnp.int32)
    key_pos = anchor - MARGIN + jnp.arange(block + 2 * MARGIN, dtype=jnp.int32)
    offsets = query_pos[:, None] - key_pos[None, :]
    inside = (key_pos >= 0) & (key_pos < seq_len)
    return (
        (jnp.abs(offsets) <= BAND)
        & inside[None, :]
        & ((key_pos < length)[None, :] | (offsets == 0))
    )


def cross(left, right):
    return lax.dot_general(
        left, right, (((0,), (0,)), ((), ())), preferred_element_type=jnp.float32
    )


def against(left, right):
    return lax.dot_general(
        left, right, (((1,), (1,)), ((), ())), preferred_element_type=jnp.float32
    )


def block_scores(query_blk, key_blk, anchor, length, seq_len, block):
    scores = (
        jnp.einsum("qhe,khe->hqk", query_blk, key_blk, preferred_element_type=jnp.float32) * 0.125
    )
    return jnp.where(band_mask(anchor, length, seq_len, block)[None], scores, -1e30)


def near_forward(query, key_pad, value_pad, length, seq_len, base, block):
    rows = query.shape[0]
    span = block + 2 * MARGIN

    def window(anchor):
        query_blk = lax.dynamic_slice_in_dim(query, anchor, block, 0)
        key_blk = lax.dynamic_slice_in_dim(key_pad, anchor, span, 0)
        value_blk = lax.dynamic_slice_in_dim(value_pad, anchor, span, 0)
        scores = block_scores(query_blk, key_blk, base + anchor, length, seq_len, block)
        row_max = jnp.max(scores, axis=-1, keepdims=True)
        exponent = jnp.exp(scores - row_max)
        summed = jnp.sum(exponent, axis=-1, keepdims=True)
        attn_probs = (exponent / summed).astype(jnp.bfloat16)
        result = jnp.einsum(
            "hqk,khe->qhe", attn_probs, value_blk, preferred_element_type=jnp.float32
        )
        return (result, (row_max + jnp.log(summed))[:, :, 0])

    anchors = jnp.arange(rows // block, dtype=jnp.int32) * block
    results, log_sums = lax.map(window, anchors)
    return (results.reshape(query.shape), log_sums)


def near_backward(query, key_pad, value_pad, grad_ctx, log_sums, length, seq_len, base, block):
    rows = query.shape[0]
    span = block + 2 * MARGIN
    padded_shape = key_pad.shape

    def visit(block_index, running):
        grad_query, grad_keys, grad_values = running
        anchor = block_index * block
        query_blk = lax.dynamic_slice_in_dim(query, anchor, block, 0)
        key_blk = lax.dynamic_slice_in_dim(key_pad, anchor, span, 0)
        value_blk = lax.dynamic_slice_in_dim(value_pad, anchor, span, 0)
        grad_blk = lax.dynamic_slice_in_dim(grad_ctx, anchor, block, 0)
        scores = block_scores(query_blk, key_blk, base + anchor, length, seq_len, block)
        attn_probs = jnp.exp(scores - log_sums[block_index][:, :, None])
        probs_low = attn_probs.astype(jnp.bfloat16)
        grad_probs = jnp.einsum(
            "qhe,khe->hqk", grad_blk, value_blk, preferred_element_type=jnp.float32
        )
        row_dot = jnp.sum(attn_probs * grad_probs, axis=-1, keepdims=True)
        grad_scores = (attn_probs * (grad_probs - row_dot)).astype(jnp.bfloat16)
        query_part = (
            jnp.einsum("hqk,khe->qhe", grad_scores, key_blk, preferred_element_type=jnp.float32)
            * 0.125
        )
        key_part = (
            jnp.einsum("hqk,qhe->khe", grad_scores, query_blk, preferred_element_type=jnp.float32)
            * 0.125
        )
        value_part = jnp.einsum(
            "hqk,qhe->khe", probs_low, grad_blk, preferred_element_type=jnp.float32
        )
        grad_query = lax.dynamic_update_slice_in_dim(grad_query, query_part, anchor, 0)
        grad_keys = lax.dynamic_update_slice_in_dim(
            grad_keys, lax.dynamic_slice_in_dim(grad_keys, anchor, span, 0) + key_part, anchor, 0
        )
        grad_values = lax.dynamic_update_slice_in_dim(
            grad_values,
            lax.dynamic_slice_in_dim(grad_values, anchor, span, 0) + value_part,
            anchor,
            0,
        )
        return (grad_query, grad_keys, grad_values)

    initial = (
        jnp.zeros(query.shape, jnp.float32),
        jnp.zeros(padded_shape, jnp.float32),
        jnp.zeros(padded_shape, jnp.float32),
    )
    return lax.fori_loop(0, rows // block, visit, initial)


def per_device(
    tokens,
    cotangent,
    lengths,
    owners,
    w_qkv,
    w_out,
    w_in,
    w_down,
    master,
    first_moment,
    second_moment,
    norm_gains,
    norm_biases,
    norm_first,
    norm_second,
):
    inputs = tokens[0].astype(jnp.float32)
    local_rows = inputs.shape[0]
    groups = lax.axis_size("mp")
    seq_len = local_rows * groups
    length = lengths[0]
    base = lax.axis_index("mp") * local_rows
    row_pos = base + jnp.arange(local_rows, dtype=jnp.int32)
    grad_output = cotangent[0].astype(jnp.float32) * (row_pos < length).astype(jnp.float32)[:, None]
    head_cols = w_out.shape[0]
    heads_dev = head_cols // HEAD
    valid_count = length.astype(jnp.float32)
    grad_mix = grad_output.astype(jnp.bfloat16)
    norm_one, norm_one_back = jax.vjp(layer_norm, inputs, norm_gains[0], norm_biases[0])
    first_local = norm_one.astype(jnp.bfloat16)
    first_all = lax.all_gather(first_local, "mp", axis=0, tiled=True)
    projected = jnp.dot(first_all, w_qkv, preferred_element_type=jnp.float32).astype(jnp.bfloat16)
    query = projected[:, :head_cols].reshape(seq_len, heads_dev, HEAD)
    keys = projected[:, head_cols : 2 * head_cols].reshape(seq_len, heads_dev, HEAD)
    values = projected[:, 2 * head_cols :].reshape(seq_len, heads_dev, HEAD)
    key_mask = (jnp.arange(seq_len, dtype=jnp.int32) < length).astype(jnp.float32)
    key_pad = jnp.pad(keys, ((MARGIN, MARGIN), (0, 0), (0, 0)))
    value_pad = jnp.pad(values, ((MARGIN, MARGIN), (0, 0), (0, 0)))
    near_part, log_sums = near_forward(query, key_pad, value_pad, length, seq_len, 0, QBLOCK)

    def far_local(query_f, keys_f, values_f):
        return far_field(query_f, keys_f, values_f, key_mask, valid_count)

    far_part, far_back = jax.vjp(
        far_local, query.astype(jnp.float32), keys.astype(jnp.float32), values.astype(jnp.float32)
    )
    context = (near_part + far_part).reshape(seq_len, head_cols).astype(jnp.bfloat16)
    second_in = inputs + lax.psum_scatter(
        jnp.dot(context, w_out, preferred_element_type=jnp.float32),
        "mp",
        scatter_dimension=0,
        tiled=True,
    )
    norm_two, norm_two_back = jax.vjp(layer_norm, second_in, norm_gains[1], norm_biases[1])
    second_local = norm_two.astype(jnp.bfloat16)
    second_all = lax.all_gather(second_local, "mp", axis=0, tiled=True)
    pre_act = jnp.dot(second_all, w_in, preferred_element_type=jnp.float32)
    activated, gelu_back = jax.vjp(jax.nn.gelu, pre_act)
    hidden = activated.astype(jnp.bfloat16)
    result = second_in + lax.psum_scatter(
        jnp.dot(hidden, w_down, preferred_element_type=jnp.float32),
        "mp",
        scatter_dimension=0,
        tiled=True,
    )
    portion = lax.all_gather(grad_mix, "mp", axis=0, tiled=True)
    grad_hidden = against(portion, w_down)
    grad_hidden, grad_down = (grad_hidden, cross(hidden, portion))
    grad_up = gelu_back(grad_hidden)[0].astype(jnp.bfloat16)
    grad_norm_two = lax.psum_scatter(against(grad_up, w_in), "mp", scatter_dimension=0, tiled=True)
    grad_inw = cross(second_all, grad_up)
    grad_second, grad_gain_two, grad_bias_two = norm_two_back(grad_norm_two)
    grad_second = grad_output + grad_second
    grad_attn = grad_second.astype(jnp.bfloat16)
    portion = lax.all_gather(grad_attn, "mp", axis=0, tiled=True)
    grad_context = against(portion, w_out)
    grad_context, grad_outw = (grad_context, cross(context, portion))
    grad_context = grad_context.astype(jnp.bfloat16).reshape(seq_len, heads_dev, HEAD)
    near_query, near_keys_pad, near_values_pad = near_backward(
        query, key_pad, value_pad, grad_context, log_sums, length, seq_len, 0, QBLOCK
    )
    near_keys = near_keys_pad[MARGIN : MARGIN + seq_len]
    near_values = near_values_pad[MARGIN : MARGIN + seq_len]
    far_query, far_keys, far_values = far_back(grad_context.astype(jnp.float32))
    grad_proj = jnp.concatenate(
        [
            (near_query + far_query).reshape(seq_len, head_cols),
            (near_keys + far_keys).reshape(seq_len, head_cols),
            (near_values + far_values).reshape(seq_len, head_cols),
        ],
        axis=1,
    ).astype(jnp.bfloat16)
    grad_norm_one = lax.psum_scatter(
        against(grad_proj, w_qkv), "mp", scatter_dimension=0, tiled=True
    )
    grad_qkvw = cross(first_all, grad_proj)
    block_rows = master.shape[1]
    grad_blocks = jnp.concatenate(
        [
            grad_qkvw.reshape(-1, 128),
            grad_outw.reshape(-1, 128),
            grad_inw.reshape(-1, 128),
            grad_down.reshape(-1, 128),
        ],
        axis=0,
    ).reshape(owners.shape[0], block_rows, 128)
    grad_first, grad_gain_one, grad_bias_one = norm_one_back(grad_norm_one)
    tokens_grad = grad_second + grad_first
    corr_one = 1.0 - beta_one**STEP
    corr_two = 1.0 - beta_two**STEP
    norm_grad = lax.psum(
        jnp.stack([grad_gain_one, grad_bias_one, grad_gain_two, grad_bias_two]), ("dp", "mp")
    )
    norm_params = jnp.stack([norm_gains[0], norm_biases[0], norm_gains[1], norm_biases[1]])
    norm_first_new = beta_one * norm_first + (1.0 - beta_one) * norm_grad
    norm_second_new = beta_two * norm_second + (1.0 - beta_two) * norm_grad * norm_grad
    norm_new = norm_params - norm_rate * (
        norm_first_new / corr_one / (jnp.sqrt(norm_second_new / corr_two) + adam_epsilon)
    )
    block_rows = master.shape[1]
    capacity = master.shape[0]
    blocks_all = owners.shape[0]
    dp_count = lax.axis_size("dp")
    onehot = (owners[:, None] == jnp.arange(dp_count, dtype=jnp.int32)[None, :]).astype(jnp.int32)
    slot_index = jnp.sum(jnp.cumsum(onehot, axis=0) * onehot, axis=1) - 1
    slot_rows = owners * capacity + slot_index
    my_rows = lax.axis_index("dp") * capacity + jnp.arange(capacity, dtype=jnp.int32)
    matches = slot_rows[None, :] == my_rows[:, None]
    filled = jnp.any(matches, axis=1)
    picked = jnp.sum(
        jnp.where(matches, jnp.arange(blocks_all, dtype=jnp.int32)[None, :], 0), axis=1
    )
    summed = lax.psum(grad_blocks, "dp")
    owned = summed[picked]
    first_upd = beta_one * first_moment + (1.0 - beta_one) * owned
    second_upd = beta_two * second_moment + (1.0 - beta_two) * owned * owned
    master_upd = master - learn_rate * (
        first_upd / corr_one / (jnp.sqrt(second_upd / corr_two) + adam_epsilon)
        + decay_rate * master
    )
    keep_mask = filled[:, None, None]
    first_new = jnp.where(keep_mask, first_upd, first_moment)
    second_new = jnp.where(keep_mask, second_upd, second_moment)
    master_new = jnp.where(keep_mask, master_upd, master)
    gathered = lax.all_gather(master_new.astype(jnp.bfloat16), "dp", axis=0, tiled=True)
    fresh = gathered[slot_rows].reshape(blocks_all * block_rows, 128)
    rows_q = w_qkv.size // 128
    rows_o = w_out.size // 128
    rows_i = w_in.size // 128
    new_qkv = fresh[:rows_q].reshape(w_qkv.shape)
    new_out = fresh[rows_q : rows_q + rows_o].reshape(w_out.shape)
    new_in = fresh[rows_q + rows_o : rows_q + rows_o + rows_i].reshape(w_in.shape)
    new_down = fresh[rows_q + rows_o + rows_i :].reshape(w_down.shape)
    return (
        result.astype(jnp.bfloat16)[None],
        tokens_grad[None],
        first_new,
        second_new,
        master_new,
        new_qkv,
        new_out,
        new_in,
        new_down,
        norm_first_new,
        norm_second_new,
        norm_new,
    )


def solution(mesh):
    return jax.shard_map(
        per_device,
        mesh=mesh,
        in_specs=(
            P("dp", "mp", None),
            P("dp", "mp", None),
            P("dp"),
            P(),
            P(None, "mp"),
            P("mp", None),
            P(None, "mp"),
            P("mp", None),
            P("dp", "mp", None),
            P("dp", "mp", None),
            P("dp", "mp", None),
            P(),
            P(),
            P(),
            P(),
        ),
        out_specs=(
            P("dp", "mp", None),
            P("dp", "mp", None),
            P("dp", "mp", None),
            P("dp", "mp", None),
            P("dp", "mp", None),
            P(None, "mp"),
            P("mp", None),
            P(None, "mp"),
            P("mp", None),
            P(),
            P(),
            P(),
        ),
        check_vma=False,
    )
```

profile of v0, /device:TPU:0, one launch (start us, length us, event | category | flops | bytes accessed | tf_op | source)
XLA Modules:
  0.0 864.3 jit_solution(8731403079336793505)
XLA Ops:
  13.6 48.1 %all-gather.6.cloned.1.call-done = bf16[2048,512]{1,0:T(8,128)(2,1)} async-done(((bf16[512,512]{1,0:T(8,128)(2,1)}), bf16[2048,512]{1,0:T(8,128)(2,1)}) %all-gather.6.cloned.1.call-update) | async-done | bytes 2097168 | tf_op jit(solution)/shard_map/all_gather | solution.py:181
  70.3 66.4 %while.33 = (s32[]{:T(128)}, f32[4,512,2,64]{1,0,3,2:T(4,128)}, f32[4,2,512]{2,1,0:T(2,128)}, s32[4]{0:T(128)S(1)}, bf16[2112,2,64]{0,2,1:T(8,128)(2,1)S(1)}, /*...) while((s32[]{:T(128)}, f32[4,512,2,64]{1,0,3,2:T(4,128)}, ...), condition=%wide.region_5.6_spmd, body=%wide.region_2.5_spmd.sunk | while | flops 160140160 | bytes 10071036 | solution.py:95
  80.7 6.1 dynamic_update_slice.52
  97.3 6.1 dynamic_update_slice.52
  113.9 6.1 dynamic_update_slice.52
  130.5 6.1 dynamic_update_slice.52
  151.2 73.6 %reduce-scatter.5.cloned.1.call-done = f32[512,512]{1,0:T(8,128)} async-done(((f32[2048,512]{1,0:T(8,128)}), f32[512,512]{1,0:T(8,128)}) %reduce-scatter.5.cloned.1.call-update) | async-done | bytes 1048592 | tf_op jit(solution)/shard_map/reduce_scatter | solution.py:198
  227.5 45.9 %all-gather.10.cloned.1.call-done = bf16[2048,512]{1,0:T(8,128)(2,1)} async-done(((bf16[512,512]{1,0:T(8,128)(2,1)}), bf16[2048,512]{1,0:T(8,128)(2,1)}) %all-gather.10.cloned.1.call-update) | async-done | bytes 2097168 | tf_op jit(solution)/shard_map/all_gather | solution.py:216
  273.4 4.8 fusion.198
  278.3 41.9 %all-gather.8.cloned.1.call-done = bf16[2048,512]{1,0:T(8,128)(2,1)} async-done(((bf16[512,512]{1,0:T(8,128)(2,1)}), bf16[2048,512]{1,0:T(8,128)(2,1)}) %all-gather.8.cloned.1.call-update) | async-done | bytes 2097168 | tf_op jit(solution)/shard_map/all_gather | solution.py:206
  320.2 6.9 fusion.53
  331.8 5.9 fusion.187
  337.8 69.6 %reduce-scatter.9.cloned.1.call-done = f32[512,512]{1,0:T(8,128)} async-done(((f32[2048,512]{1,0:T(8,128)}), f32[512,512]{1,0:T(8,128)}) %reduce-scatter.9.cloned.1.call-update) | async-done | bytes 1048592 | tf_op jit(solution)/shard_map/reduce_scatter | solution.py:220
  409.6 77.2 %reduce-scatter.7.cloned.1.call-done = f32[512,512]{1,0:T(8,128)} async-done(((f32[2048,512]{1,0:T(8,128)}), f32[512,512]{1,0:T(8,128)}) %reduce-scatter.7.cloned.1.call-update) | async-done | bytes 1048592 | tf_op jit(solution)/shard_map/reduce_scatter | solution.py:210
  496.8 4.9 fusion.186
  502.7 34.5 %all-gather.12.cloned.1.call-done = bf16[2048,512]{1,0:T(8,128)(2,1)} async-done(((bf16[512,512]{1,0:T(8,128)(2,1)}), bf16[2048,512]{1,0:T(8,128)(2,1)}) %all-gather.12.cloned.1.call-update) | async-done | bytes 2097168 | tf_op jit(solution)/shard_map/all_gather | solution.py:225
  549.5 50.3 %while.34 = (s32[]{:T(128)}, f32[2048,2,64]{0,2,1:T(8,128)}, f32[2112,2,64]{0,2,1:T(8,128)}, f32[2112,2,64]{0,2,1:T(8,128)S(1)}, bf16[2112,2,64]{0,2,1:T(8,128)(...) while((s32[]{:T(128)}, f32[2048,2,64]{0,2,1:T(8,128)}, ...), condition=%wide.region_16.17_spmd, body=%wide.region_14.16_spmd.sunk | while | flops 385149824 | bytes 24149072 | solution.py:147
  624.2 66.9 %all-reduce.4.cloned.1.call-done = f32[96,64,128]{2,1,0:T(8,128)} async-done(((f32[96,64,128]{2,1,0:T(8,128)}), f32[96,64,128]{2,1,0:T(8,128)}) %all-reduce.4.cloned.1.call-update) | async-done | bytes 3145744 | tf_op jit(solution)/shard_map/psum | solution.py:283
  693.6 4.2 fusion.189
  698.2 4.5 fusion.140
  702.7 27.7 %all-gather.14.cloned.1.call-done = bf16[192,64,128]{2,1,0:T(8,128)(2,1)} async-done(((bf16[24,64,128]{2,1,0:T(8,128)(2,1)}), bf16[192,64,128]{2,1,0:T(8,128)(2,1)}) %all-gather.14.cloned.1.call-update) | async-done | bytes 3145744 | tf_op jit(solution)/shard_map/all_gather | solution.py:295
  730.3 3.9 gather_fusion.1
  740.5 68.8 %reduce-scatter.11.cloned.1.call-done = f32[512,512]{1,0:T(8,128)} async-done(((f32[2048,512]{1,0:T(8,128)}), f32[512,512]{1,0:T(8,128)}) %reduce-scatter.11.cloned.1.call-update) | async-done | bytes 1048592 | tf_op jit(solution)/shard_map/reduce_scatter | solution.py:243
  812.9 40.8 %psum.15 = f32[4,512]{1,0:T(4,128)S(1)} all-reduce(f32[4,512]{1,0:T(4,128)S(1)} %pad_maximum_fusion.4), channel_id=1, replica_groups=mesh['dp'=8,'mp'=4] {'dp','mp'}, use_global_device_ids=true, to_apply=%region_30.31 | all-reduce | flops 2048 | bytes 16384 | tf_op jit(solution)/shard_map/psum | solution.py:261
  (319 shorter events, 177.2 us)
Async XLA Ops:
  7.2 313.0 %copy-start = (bf16[512,512]{1,0:T(8,128)(2,1)S(1)}, bf16[512,512]{1,0:T(8,128)(2,1)}, u32[]{:S(2)}) copy-start(bf16[512,512]{1,0:T(8,128)(2,1)} %param.25) | copy-start | bytes 1572868
  7.2 54.4 %all-gather.6.cloned.1.call-start = ((), (), s32[]{:S(2)}) async-start(), calls=%async_computation.4 | async-start | bytes 2621440 | tf_op jit(solution)/shard_map/all_gather | solution.py:181
  10.7 215.7 %copy-start.35 = (f32[1,512]{1,0:T(1,128)}, f32[1,512]{1,0:T(1,128)S(1)}, u32[]{:S(2)}) copy-start(f32[1,512]{1,0:T(1,128)S(1)} %get-tuple-element.443) | copy-start | bytes 6148
  10.7 476.1 %copy-start.25 = (f32[1,512]{1,0:T(1,128)}, f32[1,512]{1,0:T(1,128)S(1)}, u32[]{:S(2)}) copy-start(f32[1,512]{1,0:T(1,128)S(1)} %get-tuple-element.434) | copy-start | bytes 6148
  12.8 211.9 %reduce-scatter.5.cloned.1.call-start = ((), (), s32[]{:S(2)}) async-start(), calls=%async_computation.5 | async-start | bytes 5242880 | tf_op jit(solution)/shard_map/reduce_scatter | solution.py:198
  149.1 75.7 %copy-start.2 = (bf16[1,512,512]{2,1,0:T(8,128)(2,1)S(1)}, bf16[1,512,512]{2,1,0:T(8,128)(2,1)}, u32[]{:S(2)}) copy-start(bf16[1,512,512]{2,1,0:T(8,128)(2,1)} %param.19) | copy-start | bytes 1572868
  149.1 124.3 %all-gather.10.cloned.1.call-start = ((), (), s32[]{:S(2)}) async-start(), calls=%async_computation.8 | async-start | bytes 2621440 | tf_op jit(solution)/shard_map/all_gather | solution.py:216
  150.1 339.5 %copy-start.29 = (f32[512]{0:T(512)}, f32[512]{0:T(512)S(1)}, u32[]{:S(2)}) copy-start(f32[512]{0:T(512)S(1)} %fusion.167) | copy-start | bytes 6148
  151.1 122.3 %copy-start.20 = (bf16[512,512]{1,0:T(8,128)(2,1)S(1)}, bf16[512,512]{1,0:T(8,128)(2,1)}, u32[]{:S(2)}) copy-start(bf16[512,512]{1,0:T(8,128)(2,1)} %param.26) | copy-start | bytes 1572868
  151.1 169.1 %all-gather.8.cloned.1.call-start = ((), (), s32[]{:S(2)}) async-start(), calls=%async_computation.6 | async-start | bytes 2621440 | tf_op jit(solution)/shard_map/all_gather | solution.py:206
  227.5 179.9 %reduce-scatter.9.cloned.1.call-start = ((), (), s32[]{:S(2)}) async-start(), calls=%async_computation.9 | async-start | bytes 5242880 | tf_op jit(solution)/shard_map/reduce_scatter | solution.py:220
  331.7 155.1 %reduce-scatter.7.cloned.1.call-start = ((), (), s32[]{:S(2)}) async-start(), calls=%async_computation.7 | async-start | bytes 5242880 | tf_op jit(solution)/shard_map/reduce_scatter | solution.py:210
  337.7 199.5 %all-gather.12.cloned.1.call-start = ((), (), s32[]{:S(2)}) async-start(), calls=%async_computation.10 | async-start | bytes 2621440 | tf_op jit(solution)/shard_map/all_gather | solution.py:225
  409.6 80.0 %copy-start.11 = (bf16[1,512,512]{2,1,0:T(8,128)(2,1)S(1)}, bf16[1,512,512]{2,1,0:T(8,128)(2,1)}, u32[]{:S(2)}) copy-start(bf16[1,512,512]{2,1,0:T(8,128)(2,1)} %param.20) | copy-start | bytes 1572868
  490.7 200.4 %all-reduce.4.cloned.1.call-start = ((), (), s32[]{:S(2)}) async-start(), calls=%async_computation.12 | async-start | bytes 6291456 | tf_op jit(solution)/shard_map/psum | solution.py:283
  622.7 107.6 %all-gather.14.cloned.1.call-start = ((), (), s32[]{:S(2)}) async-start(), calls=%async_computation.13 | async-start | bytes 3538944 | tf_op jit(solution)/shard_map/all_gather | solution.py:295
  697.8 111.5 %reduce-scatter.11.cloned.1.call-start = ((), (), s32[]{:S(2)}) async-start(), calls=%async_computation.11 | async-start | bytes 5242880 | tf_op jit(solution)/shard_map/reduce_scatter | solution.py:243
  738.4 115.3 %copy-start.26 = (f32[1,512]{1,0:T(1,128)S(1)}, f32[1,512]{1,0:T(1,128)}, u32[]{:S(2)}) copy-start(f32[1,512]{1,0:T(1,128)} %copy-done.25) | copy-start | bytes 6148
  738.4 115.3 %copy-start.34 = (f32[1,512]{1,0:T(1,128)S(1)}, f32[1,512]{1,0:T(1,128)}, u32[]{:S(2)}) copy-start(f32[1,512]{1,0:T(1,128)} %copy-done.33) | copy-start | bytes 6148
  738.4 115.3 %copy-start.36 = (f32[1,512]{1,0:T(1,128)S(1)}, f32[1,512]{1,0:T(1,128)}, u32[]{:S(2)}) copy-start(f32[1,512]{1,0:T(1,128)} %copy-done.35) | copy-start | bytes 6148
  738.4 115.3 %copy-start.42 = (f32[4,512]{1,0:T(4,128)S(1)}, f32[4,512]{1,0:T(4,128)}, u32[]{:S(2)}) copy-start(f32[4,512]{1,0:T(4,128)} %param.33) | copy-start | bytes 24580
  738.4 115.3 %copy-start.43 = (f32[4,512]{1,0:T(4,128)S(1)}, f32[4,512]{1,0:T(4,128)}, u32[]{:S(2)}) copy-start(f32[4,512]{1,0:T(4,128)} %param.32) | copy-start | bytes 24580
  739.3 115.0 %copy-start.30 = (f32[512]{0:T(512)S(1)}, f32[512]{0:T(512)}, u32[]{:S(2)}) copy-start(f32[512]{0:T(512)} %copy-done.29) | copy-start | bytes 6148
  739.3 115.0 %copy-start.38 = (f32[512]{0:T(512)S(1)}, f32[512]{0:T(512)}, u32[]{:S(2)}) copy-start(f32[512]{0:T(512)} %copy-done.37) | copy-start | bytes 6148
  (47 other events, 1018.0 us)
Sparse Core Ops, SparseCore 0:
  13.0 48.6 all-gather.5
  149.2 75.4 reduce-scatter.4
  227.0 46.4 all-gather.9
  275.5 44.6 all-gather.7
  331.9 75.4 reduce-scatter.8
  409.5 77.2 reduce-scatter.6
  490.8 46.3 all-gather.11
  622.9 68.1 all-reduce.3
  697.9 32.3 all-gather.13
  732.5 76.7 reduce-scatter.10
where the time goes:
time: 876 us; the launch traced here: 864 us
  waiting for transfers between devices  554 us (63%)
  matrix products  115 us (13%)
  local copies, waits for them, and re-layouts  69.2 us (8%)
  other arithmetic  51.3 us (6%)
  blocking collectives  40.8 us (5%)
  loops' own time  16.4 us (2%)
  between operations  16.1 us (2%)
    reduce_scatter x1, waiting for transfers between devices, per_device(): lax.psum_scatter(jnp.dot(hidden, w_down, preferred_element_type=jnp.float...  77.2 us
    reduce_scatter x1, waiting for transfers between devices, per_device(): lax.psum_scatter(jnp.dot(context, w_out, preferred_element_type=jnp.float...  73.6 us
    reduce_scatter x1, waiting for transfers between devices, per_device(): lax.psum_scatter(against(grad_up, w_in), 'mp', scatter_dimension=0, tiled...  69.6 us
    reduce_scatter x1, waiting for transfers between devices, per_device(): lax.psum_scatter(against(grad_proj, w_qkv), 'mp', scatter_dimension=0, ti...  68.8 us
    psum x1, waiting for transfers between devices, per_device(): summed = lax.psum(grad_blocks, 'dp')  66.9 us
    all_gather x1, waiting for transfers between devices, per_device(): first_all = lax.all_gather(first_local, 'mp', axis=0, tiled=True)  48.1 us
    all_gather x1, waiting for transfers between devices, per_device(): portion = lax.all_gather(grad_mix, 'mp', axis=0, tiled=True)  45.9 us
    all_gather x1, waiting for transfers between devices, per_device(): second_all = lax.all_gather(second_local, 'mp', axis=0, tiled=True)  41.9 us
  transfers between devices with their start and end apart: 10, of which 10 were waited for; matrix products, arithmetic and copies ran while one was open for 5% of the time, Pallas kernels for 0%

commit v1 on v0

--- a/solution.py
+++ b/solution.py
@@ -258,8 +258,11 @@
     tokens_grad = grad_second + grad_first
     corr_one = 1.0 - beta_one**STEP
     corr_two = 1.0 - beta_two**STEP
-    norm_grad = lax.psum(
-        jnp.stack([grad_gain_one, grad_bias_one, grad_gain_two, grad_bias_two]), ("dp", "mp")
+    norm_grad = jnp.sum(
+        lax.all_gather(
+            jnp.stack([grad_gain_one, grad_bias_one, grad_gain_two, grad_bias_two]), ("dp", "mp")
+        ),
+        axis=0,
     )
     norm_params = jnp.stack([norm_gains[0], norm_biases[0], norm_gains[1], norm_biases[1]])
     norm_first_new = beta_one * norm_first + (1.0 - beta_one) * norm_grad

time: 876 us -> 905 us (1.033)
  blocking collectives: 40.8 us -> 69.6 us
    all_gather x0 -> x1, blocking collectives: none -> 69.6 us  [per_device(): lax.all_gather(jnp.stack([grad_gain_one, grad_bias_one, grad_gain_two, gr...]
    psum x1 -> x0, blocking collectives: 40.8 us -> none  [per_device(): lax.psum(jnp.stack([grad_gain_one, grad_bias_one, grad_gain_two, grad_bia...]
where the time goes in v1:
time: 905 us; the launch traced here: 893 us
  waiting for transfers between devices  554 us (61%)
  matrix products  115 us (13%)
  blocking collectives  69.6 us (8%)
  local copies, waits for them, and re-layouts  69.2 us (8%)
  other arithmetic  51.3 us (6%)
  loops' own time  16.4 us (2%)
  between operations  16.1 us (2%)
    reduce_scatter x1, waiting for transfers between devices, per_device(): lax.psum_scatter(jnp.dot(hidden, w_down, preferred_element_type=jnp.float...  77.2 us
    reduce_scatter x1, waiting for transfers between devices, per_device(): lax.psum_scatter(jnp.dot(context, w_out, preferred_element_type=jnp.float...  73.6 us
    all_gather x1, blocking collectives, per_device(): lax.all_gather(jnp.stack([grad_gain_one, grad_bias_one, grad_gain_two, gr...  69.6 us
    reduce_scatter x1, waiting for transfers between devices, per_device(): lax.psum_scatter(against(grad_up, w_in), 'mp', scatter_dimension=0, tiled...  69.6 us
    reduce_scatter x1, waiting for transfers between devices, per_device(): lax.psum_scatter(against(grad_proj, w_qkv), 'mp', scatter_dimension=0, ti...  68.8 us
    psum x1, waiting for transfers between devices, per_device(): summed = lax.psum(grad_blocks, 'dp')  66.9 us
    all_gather x1, waiting for transfers between devices, per_device(): first_all = lax.all_gather(first_local, 'mp', axis=0, tiled=True)  48.1 us
    all_gather x1, waiting for transfers between devices, per_device(): portion = lax.all_gather(grad_mix, 'mp', axis=0, tiled=True)  45.9 us
  transfers between devices with their start and end apart: 10, of which 10 were waited for; matrix products, arithmetic and copies ran while one was open for 5% of the time, Pallas kernels for 0%

profile of v1, /device:TPU:0, one launch (start us, length us, event | category | flops | bytes accessed | tf_op | source)
XLA Modules:
  0.0 893.1 jit_solution(6082488349117285246)
XLA Ops:
  13.6 48.1 %all-gather.8.cloned.1.call-done = bf16[2048,512]{1,0:T(8,128)(2,1)} async-done(((bf16[512,512]{1,0:T(8,128)(2,1)}), bf16[2048,512]{1,0:T(8,128)(2,1)}) %all-gather.8.cloned.1.call-update) | async-done | bytes 2097168 | tf_op jit(solution)/shard_map/all_gather | solution.py:181
  70.3 66.4 %while.33 = (s32[]{:T(128)}, f32[4,512,2,64]{1,0,3,2:T(4,128)}, f32[4,2,512]{2,1,0:T(2,128)}, s32[4]{0:T(128)S(1)}, bf16[2112,2,64]{0,2,1:T(8,128)(2,1)S(1)}, /*...) while((s32[]{:T(128)}, f32[4,512,2,64]{1,0,3,2:T(4,128)}, ...), condition=%wide.region_5.6_spmd, body=%wide.region_2.5_spmd.sunk | while | flops 160140160 | bytes 10071036 | solution.py:95
  80.7 6.1 dynamic_update_slice.52
  97.3 6.1 dynamic_update_slice.52
  113.9 6.1 dynamic_update_slice.52
  130.5 6.1 dynamic_update_slice.52
  151.2 73.6 %reduce-scatter.5.cloned.1.call-done = f32[512,512]{1,0:T(8,128)} async-done(((f32[2048,512]{1,0:T(8,128)}), f32[512,512]{1,0:T(8,128)}) %reduce-scatter.5.cloned.1.call-update) | async-done | bytes 1048592 | tf_op jit(solution)/shard_map/reduce_scatter | solution.py:198
  227.5 45.9 %all-gather.12.cloned.1.call-done = bf16[2048,512]{1,0:T(8,128)(2,1)} async-done(((bf16[512,512]{1,0:T(8,128)(2,1)}), bf16[2048,512]{1,0:T(8,128)(2,1)}) %all-gather.12.cloned.1.call-update) | async-done | bytes 2097168 | tf_op jit(solution)/shard_map/all_gather | solution.py:216
  273.4 4.8 fusion.198
  278.3 41.9 %all-gather.10.cloned.1.call-done = bf16[2048,512]{1,0:T(8,128)(2,1)} async-done(((bf16[512,512]{1,0:T(8,128)(2,1)}), bf16[2048,512]{1,0:T(8,128)(2,1)}) %all-gather.10.cloned.1.call-update) | async-done | bytes 2097168 | tf_op jit(solution)/shard_map/all_gather | solution.py:206
  320.2 6.9 fusion.53
  331.8 5.9 fusion.187
  337.8 69.6 %reduce-scatter.9.cloned.1.call-done = f32[512,512]{1,0:T(8,128)} async-done(((f32[2048,512]{1,0:T(8,128)}), f32[512,512]{1,0:T(8,128)}) %reduce-scatter.9.cloned.1.call-update) | async-done | bytes 1048592 | tf_op jit(solution)/shard_map/reduce_scatter | solution.py:220
  409.6 77.2 %reduce-scatter.7.cloned.1.call-done = f32[512,512]{1,0:T(8,128)} async-done(((f32[2048,512]{1,0:T(8,128)}), f32[512,512]{1,0:T(8,128)}) %reduce-scatter.7.cloned.1.call-update) | async-done | bytes 1048592 | tf_op jit(solution)/shard_map/reduce_scatter | solution.py:210
  496.8 4.9 fusion.186
  502.7 34.5 %all-gather.14.cloned.1.call-done = bf16[2048,512]{1,0:T(8,128)(2,1)} async-done(((bf16[512,512]{1,0:T(8,128)(2,1)}), bf16[2048,512]{1,0:T(8,128)(2,1)}) %all-gather.14.cloned.1.call-update) | async-done | bytes 2097168 | tf_op jit(solution)/shard_map/all_gather | solution.py:225
  549.5 50.3 %while.34 = (s32[]{:T(128)}, f32[2048,2,64]{0,2,1:T(8,128)}, f32[2112,2,64]{0,2,1:T(8,128)}, f32[2112,2,64]{0,2,1:T(8,128)S(1)}, bf16[2112,2,64]{0,2,1:T(8,128)(...) while((s32[]{:T(128)}, f32[2048,2,64]{0,2,1:T(8,128)}, ...), condition=%wide.region_16.17_spmd, body=%wide.region_14.16_spmd.sunk | while | flops 385149824 | bytes 24149072 | solution.py:147
  624.2 66.9 %all-reduce.4.cloned.1.call-done = f32[96,64,128]{2,1,0:T(8,128)} async-done(((f32[96,64,128]{2,1,0:T(8,128)}), f32[96,64,128]{2,1,0:T(8,128)}) %all-reduce.4.cloned.1.call-update) | async-done | bytes 3145744 | tf_op jit(solution)/shard_map/psum | solution.py:286
  693.6 4.2 fusion.189
  698.2 4.5 fusion.140
  702.7 27.7 %all-gather.16.cloned.1.call-done = bf16[192,64,128]{2,1,0:T(8,128)(2,1)} async-done(((bf16[24,64,128]{2,1,0:T(8,128)(2,1)}), bf16[192,64,128]{2,1,0:T(8,128)(2,1)}) %all-gather.16.cloned.1.call-update) | async-done | bytes 3145744 | tf_op jit(solution)/shard_map/all_gather | solution.py:298
  730.3 3.9 gather_fusion.1
  740.4 68.8 %reduce-scatter.11.cloned.1.call-done = f32[512,512]{1,0:T(8,128)} async-done(((f32[2048,512]{1,0:T(8,128)}), f32[512,512]{1,0:T(8,128)}) %reduce-scatter.11.cloned.1.call-update) | async-done | bytes 1048592 | tf_op jit(solution)/shard_map/reduce_scatter | solution.py:243
  812.8 69.6 %all-gather.1 = f32[32,4,512]{2,1,0:T(4,128)S(1)} all-gather(f32[1,4,512]{2,1,0:T(4,128)S(1)} %maximum_bitcast_fusion), channel_id=2, replica_groups=mesh['dp'=8,'mp'=4] {'dp','mp'}, dimensions={0}, use_global_device_ids=true | all-gather | bytes 270336 | tf_op jit(solution)/shard_map/all_gather | solution.py:262
  (320 shorter events, 177.2 us)
Async XLA Ops:
  7.2 313.0 %copy-start = (bf16[512,512]{1,0:T(8,128)(2,1)S(1)}, bf16[512,512]{1,0:T(8,128)(2,1)}, u32[]{:S(2)}) copy-start(bf16[512,512]{1,0:T(8,128)(2,1)} %param.25) | copy-start | bytes 1572868
  7.2 54.4 %all-gather.8.cloned.1.call-start = ((), (), s32[]{:S(2)}) async-start(), calls=%async_computation.4 | async-start | bytes 2621440 | tf_op jit(solution)/shard_map/all_gather | solution.py:181
  10.7 215.7 %copy-start.35 = (f32[1,512]{1,0:T(1,128)}, f32[1,512]{1,0:T(1,128)S(1)}, u32[]{:S(2)}) copy-start(f32[1,512]{1,0:T(1,128)S(1)} %get-tuple-element.443) | copy-start | bytes 6148
  10.7 476.1 %copy-start.25 = (f32[1,512]{1,0:T(1,128)}, f32[1,512]{1,0:T(1,128)S(1)}, u32[]{:S(2)}) copy-start(f32[1,512]{1,0:T(1,128)S(1)} %get-tuple-element.434) | copy-start | bytes 6148
  12.8 211.9 %reduce-scatter.5.cloned.1.call-start = ((), (), s32[]{:S(2)}) async-start(), calls=%async_computation.5 | async-start | bytes 5242880 | tf_op jit(solution)/shard_map/reduce_scatter | solution.py:198
  149.1 75.7 %copy-start.2 = (bf16[1,512,512]{2,1,0:T(8,128)(2,1)S(1)}, bf16[1,512,512]{2,1,0:T(8,128)(2,1)}, u32[]{:S(2)}) copy-start(bf16[1,512,512]{2,1,0:T(8,128)(2,1)} %param.19) | copy-start | bytes 1572868
  149.1 124.3 %all-gather.12.cloned.1.call-start = ((), (), s32[]{:S(2)}) async-start(), calls=%async_computation.8 | async-start | bytes 2621440 | tf_op jit(solution)/shard_map/all_gather | solution.py:216
  150.1 339.5 %copy-start.29 = (f32[512]{0:T(512)}, f32[512]{0:T(512)S(1)}, u32[]{:S(2)}) copy-start(f32[512]{0:T(512)S(1)} %fusion.167) | copy-start | bytes 6148
  151.1 122.3 %copy-start.20 = (bf16[512,512]{1,0:T(8,128)(2,1)S(1)}, bf16[512,512]{1,0:T(8,128)(2,1)}, u32[]{:S(2)}) copy-start(bf16[512,512]{1,0:T(8,128)(2,1)} %param.26) | copy-start | bytes 1572868
  151.1 169.1 %all-gather.10.cloned.1.call-start = ((), (), s32[]{:S(2)}) async-start(), calls=%async_computation.6 | async-start | bytes 2621440 | tf_op jit(solution)/shard_map/all_gather | solution.py:206
  227.5 179.9 %reduce-scatter.9.cloned.1.call-start = ((), (), s32[]{:S(2)}) async-start(), calls=%async_computation.9 | async-start | bytes 5242880 | tf_op jit(solution)/shard_map/reduce_scatter | solution.py:220
  331.7 155.1 %reduce-scatter.7.cloned.1.call-start = ((), (), s32[]{:S(2)}) async-start(), calls=%async_computation.7 | async-start | bytes 5242880 | tf_op jit(solution)/shard_map/reduce_scatter | solution.py:210
  337.7 199.5 %all-gather.14.cloned.1.call-start = ((), (), s32[]{:S(2)}) async-start(), calls=%async_computation.10 | async-start | bytes 2621440 | tf_op jit(solution)/shard_map/all_gather | solution.py:225
  409.6 80.0 %copy-start.11 = (bf16[1,512,512]{2,1,0:T(8,128)(2,1)S(1)}, bf16[1,512,512]{2,1,0:T(8,128)(2,1)}, u32[]{:S(2)}) copy-start(bf16[1,512,512]{2,1,0:T(8,128)(2,1)} %param.20) | copy-start | bytes 1572868
  490.7 200.4 %all-reduce.4.cloned.1.call-start = ((), (), s32[]{:S(2)}) async-start(), calls=%async_computation.12 | async-start | bytes 6291456 | tf_op jit(solution)/shard_map/psum | solution.py:286
  622.7 107.6 %all-gather.16.cloned.1.call-start = ((), (), s32[]{:S(2)}) async-start(), calls=%async_computation.13 | async-start | bytes 3538944 | tf_op jit(solution)/shard_map/all_gather | solution.py:298
  697.8 111.5 %reduce-scatter.11.cloned.1.call-start = ((), (), s32[]{:S(2)}) async-start(), calls=%async_computation.11 | async-start | bytes 5242880 | tf_op jit(solution)/shard_map/reduce_scatter | solution.py:243
  739.3 143.2 %copy-start.26 = (f32[1,512]{1,0:T(1,128)S(1)}, f32[1,512]{1,0:T(1,128)}, u32[]{:S(2)}) copy-start(f32[1,512]{1,0:T(1,128)} %copy-done.25) | copy-start | bytes 6148
  739.3 143.2 %copy-start.34 = (f32[1,512]{1,0:T(1,128)S(1)}, f32[1,512]{1,0:T(1,128)}, u32[]{:S(2)}) copy-start(f32[1,512]{1,0:T(1,128)} %copy-done.33) | copy-start | bytes 6148
  739.3 143.2 %copy-start.36 = (f32[1,512]{1,0:T(1,128)S(1)}, f32[1,512]{1,0:T(1,128)}, u32[]{:S(2)}) copy-start(f32[1,512]{1,0:T(1,128)} %copy-done.35) | copy-start | bytes 6148
  739.3 143.2 %copy-start.42 = (f32[4,512]{1,0:T(4,128)S(1)}, f32[4,512]{1,0:T(4,128)}, u32[]{:S(2)}) copy-start(f32[4,512]{1,0:T(4,128)} %param.33) | copy-start | bytes 24580
  739.3 143.2 %copy-start.43 = (f32[4,512]{1,0:T(4,128)S(1)}, f32[4,512]{1,0:T(4,128)}, u32[]{:S(2)}) copy-start(f32[4,512]{1,0:T(4,128)} %param.32) | copy-start | bytes 24580
  739.3 143.9 %copy-start.30 = (f32[512]{0:T(512)S(1)}, f32[512]{0:T(512)}, u32[]{:S(2)}) copy-start(f32[512]{0:T(512)} %copy-done.29) | copy-start | bytes 6148
  739.3 143.8 %copy-start.38 = (f32[512]{0:T(512)S(1)}, f32[512]{0:T(512)}, u32[]{:S(2)}) copy-start(f32[512]{0:T(512)} %copy-done.37) | copy-start | bytes 6148
  (47 other events, 1073.6 us)
Sparse Core Ops, SparseCore 0:
  13.0 48.6 all-gather.7
  149.2 75.4 reduce-scatter.4
  227.0 46.4 all-gather.11
  275.5 44.6 all-gather.9
  331.9 75.4 reduce-scatter.8
  409.5 77.2 reduce-scatter.6
  490.8 46.3 all-gather.13
  622.9 68.1 all-reduce.3
  697.9 32.3 all-gather.15
  732.5 76.7 reduce-scatter.10
